TPU v7x, 32 devices: a whole 2x2x4 slice. The times are simulated.
32 devices in a mesh: rows: 8 (over z, x), ch: 4 (over y, core).
Axes of the slice: x: 2, y: 2, z: 4, core: 2. Of those that a mesh axis runs over, the one named last changes fastest.
Arguments:
- features: bfloat16 [64, 4096], P('ch', 'rows'), may hold values from -6 to 6
- tiles: bfloat16 [32, 20, 128, 128], P('rows'), may hold values from -0.0625 to 0.0625
- tile_cols: int32 [32, 20], P('rows'), may hold values from 0 to 11, as said below
- needs: int32 [8, 8, 1], P('rows'), may hold values from -1 to 3, as said below
- weights: bfloat16 [4, 64, 64], P(None, 'ch'), may hold values from -0.375 to 0.375
- cotangent: bfloat16 [64, 4096], P('ch', 'rows'), may hold values from -6 to 6
Outputs:
- output: bfloat16 [64, 4096], P('ch', 'rows')
- feature_grad: bfloat16 [64, 4096], P('ch', 'rows')
- weight_grad: float32 [4, 64, 64], P(None, 'ch')
Inputs may be any that keep to these rules, and one draw needn't show every extreme that they name: needs[d, o, s] is a block index of device o, or -1 where unset; row o = d is unset; slot 0 is set for every o other than d; the set entries of one (d, o) differ; some device o has all 1 slots set by every other device. `tile_cols`: the first tile of row block b is its own block (entry b mod 4); an entry v >= 4 names cell v - 4 = 1 o + s with needs[d, o, s] set; every set entry of needs[d] is named by some tile of device d.
All inputs are finite; a program needn't handle non-finite values.
Results may differ from a plain program's by a relative error of at most 0.0055.
Values may be sent and summed in bfloat16 or wider, within the bound.
No kernel may reach another device: no remote copies, remote signals or barrier semaphores. Data moves between devices by JAX's collectives and lax.ppermute only.
A program may use at most 64 MiB of HBM per device.

v0:
```python
import jax
import jax.numpy as jnp
from jax import lax
from jax.sharding import PartitionSpec as P

K = 4


def body(features, tiles, tile_cols, needs, weights, cotangent):
    channels = features.shape[0]
    node_count = features.shape[1]
    blocks = tiles.shape[0]
    per_row = tiles.shape[1]
    block_width = tiles.shape[2]
    slot_count = needs.shape[2]
    shards = lax.axis_size("rows")
    flat_cols = tile_cols.reshape(-1)
    position = lax.axis_index("rows")
    ghost_cell = jnp.clip(flat_cols - blocks, 0, shards * slot_count - 1)
    needed = needs[0].reshape(-1)[ghost_cell]
    remote = ghost_cell // slot_count * blocks + jnp.maximum(needed, 0)
    source_index = jnp.where(flat_cols < blocks, position * blocks + flat_cols, remote)
    extent = blocks * shards

    def gather_source(values):
        return lax.all_gather(values, "rows", axis=1, tiled=True)

    def return_partials(partials):
        return lax.psum_scatter(partials, "rows", scatter_dimension=1, tiled=True)

    def forward_apply(term):
        source = gather_source(term.reshape(channels, blocks, block_width))
        picked = source[:, source_index, :].reshape(channels, blocks, per_row, block_width)
        result = jnp.einsum("crtj,rtij->cri", picked, tiles, preferred_element_type=jnp.float32)
        return result.reshape(channels, node_count)

    def transposed_apply(rounded):
        shaped = rounded.reshape(channels, blocks, block_width)
        contrib = jnp.einsum("cri,rtij->crtj", shaped, tiles, preferred_element_type=jnp.float32)
        contrib = contrib.reshape(channels, blocks * per_row, block_width)
        partials = (
            jnp.zeros((channels, extent, block_width), jnp.float32)
            .at[:, source_index, :]
            .add(contrib)
        )
        return return_partials(partials).reshape(channels, node_count)

    cheb_terms = [features, forward_apply(features).astype(jnp.bfloat16)]
    for degree in range(2, K):
        latest = 2.0 * forward_apply(cheb_terms[-1]) - cheb_terms[-2].astype(jnp.float32)
        cheb_terms.append(latest.astype(jnp.bfloat16))
    stacked = jnp.stack(cheb_terms)
    output = lax.psum_scatter(
        jnp.einsum("kio,kin->on", weights, stacked, preferred_element_type=jnp.float32),
        "ch",
        scatter_dimension=0,
        tiled=True,
    ).astype(jnp.bfloat16)
    grad_out = lax.all_gather(cotangent, "ch", axis=0, tiled=True)
    local_wgrad = jnp.einsum("kin,on->kio", stacked, grad_out, preferred_element_type=jnp.float32)
    weight_grad = lax.psum(local_wgrad, "rows")
    term_grads = jnp.einsum("kio,on->kin", weights, grad_out, preferred_element_type=jnp.float32)
    adjoints = [term_grads[degree] for degree in range(K)]
    for degree in range(K - 1, 1, -1):
        rounded = adjoints[degree].astype(jnp.bfloat16)
        adjoints[degree - 1] = adjoints[degree - 1] + 2.0 * transposed_apply(rounded)
        adjoints[degree - 2] = adjoints[degree - 2] - adjoints[degree]
    last = transposed_apply(adjoints[1].astype(jnp.bfloat16))
    feature_grad = (adjoints[0] + last).astype(jnp.bfloat16)
    return (output, feature_grad, weight_grad)


def solution(mesh):
    placed = (
        P("ch", "rows"),
        P("rows", None, None, None),
        P("rows", None),
        P("rows", None, None),
        P(None, "ch", None),
        P("ch", "rows"),
    )
    return jax.shard_map(
        body,
        mesh=mesh,
        in_specs=placed,
        out_specs=(P("ch", "rows"), P("ch", "rows"), P(None, "ch", None)),
        check_vma=False,
    )
```

profile of v0, /device:TPU:0, one launch (start us, length us, event | category | flops | bytes accessed | tf_op | source)
XLA Modules:
  0.0 292.1 jit_solution(1852419735173445717)
XLA Ops:
  7.2 1.6 fusion.37
  10.5 6.4 %all_gather.15 = bf16[64,512]{1,0:T(8,128)(2,1)S(1)} all-gather(bf16[16,512]{1,0:T(8,128)(2,1)} %param.11), channel_id=1, replica_groups=mesh['rows'=8,'ch'=4] {'ch'}, dimensions={0}, use_global_device_ids=true | all-gather | bytes 81920 | tf_op jit(solution)/shard_map/all_gather | solution.py:59
  17.6 0.8 fusion.8
  19.6 5.7 %fusion.30 = s32[80]{0:T(128)} fusion(pred[80,1]{0,1:T(4,128)(4,1)S(1)} %lt.31, s32[80,1]{0,1:T(1,128)S(1)} %add.100, s32[80,1]{0,1:T(1,128)S(1)} %min.12, s32[]{:T(128)} %bitcast.3, s32[]{:T(128)} %bitcast.4, s32[]{:T(128)} %bitcast.5, s32[]{:T(128)} %bitcast.6, s32[]{:T(128)} %bitcast.7, s32[]{:T(128)} %bitcast.9, s32[]{:T(128)} %bitcast.8, s32[]{:T(128)} %bitcast.2), kind=kLoop, calls=%fused_computation.64 | loop fusion | flops 1920 | bytes 1072 | tf_op jit(solution)/shard_map/select_n | solution.py:33
  25.2 3.7 %scatter_fusion = f32[16,32,128]{2,0,1:T(8,128)S(1)} fusion(f32[16,32,128]{2,0,1:T(8,128)S(1)} %broadcast.155.clone, s32[80]{0:T(128)} %fusion.30, f32[80,16,128]{2,1,0:T(8,128)S(1)} %bitcast.172), kind=kCustom, calls=%fused_computation.3 | custom fusion | flops 163840 | bytes 1966400 | tf_op jit(solution)/shard_map/scatter-add | solution.py:44
  29.7 1.4 slice_subtract_fusion
  31.8 31.4 %all_gather.12 = bf16[16,32,128]{2,0,1:T(8,128)(2,1)S(1)} all-gather(bf16[16,4,128]{2,0,1:T(8,128)(2,1)S(1)} %copy_bitcast_fusion.1), channel_id=1, replica_groups=mesh['rows'=8,'ch'=4] {'rows'}, dimensions={1}, use_global_device_ids=true | all-gather | bytes 147456 | tf_op jit(solution)/shard_map/all_gather | solution.py:26
  63.8 0.8 fusion.5
  64.6 30.6 %all_gather.13 = bf16[16,32,128]{2,0,1:T(8,128)(2,1)S(1)} all-gather(bf16[16,4,128]{2,0,1:T(8,128)(2,1)S(1)} %fusion.5), channel_id=1, replica_groups=mesh['rows'=8,'ch'=4] {'rows'}, dimensions={1}, use_global_device_ids=true | all-gather | bytes 147456 | tf_op jit(solution)/shard_map/all_gather | solution.py:26
  97.0 0.8 fusion.3
  98.5 30.5 %all_gather.14 = bf16[16,32,128]{2,0,1:T(8,128)(2,1)S(1)} all-gather(bf16[16,4,128]{2,0,1:T(8,128)(2,1)S(1)} %bitcast.179), channel_id=1, replica_groups=mesh['rows'=8,'ch'=4] {'rows'}, dimensions={1}, use_global_device_ids=true | all-gather | bytes 147456 | tf_op jit(solution)/shard_map/all_gather | solution.py:26
  129.0 1.4 gather_fusion.2
  130.3 1.2 fusion.16
  131.6 3.7 %scatter_fusion.1 = f32[16,32,128]{2,0,1:T(8,128)S(1)} fusion(f32[16,32,128]{2,0,1:T(8,128)S(1)} %broadcast.155.clone.1, s32[80]{0:T(128)} %fusion.30, f32[80,16,128]{2,1,0:T(8,128)S(1)} %bitcast.171), kind=kCustom, calls=%fused_computation.4 | custom fusion | flops 163840 | bytes 1966400 | tf_op jit(solution)/shard_map/scatter-add | solution.py:44
  136.1 1.7 fusion.1
  138.0 0.9 convolution_bitcast_fusion
  138.9 59.3 %reduce-scatter.9.cloned.1.call-done = f32[16,4,128]{2,0,1:T(8,128)} async-done(((f32[16,32,128]{2,0,1:T(8,128)}), f32[16,4,128]{2,0,1:T(8,128)}) %reduce-scatter.9.cloned.1.call-update) | async-done | bytes 32784 | tf_op jit(solution)/shard_map/reduce_scatter | solution.py:29
  198.3 1.2 fusion.19
  199.5 3.7 %scatter_fusion.2 = f32[16,32,128]{2,0,1:T(8,128)S(1)} fusion(f32[16,32,128]{2,0,1:T(8,128)S(1)} %broadcast.155, s32[80]{0:T(128)} %fusion.30, f32[80,16,128]{2,1,0:T(8,128)S(1)} %bitcast.170), kind=kCustom, calls=%fused_computation.5 | custom fusion | flops 163840 | bytes 1966400 | tf_op jit(solution)/shard_map/scatter-add | solution.py:44
  203.9 1.0 fusion.6
  205.0 35.8 %psum.7 = f32[4,16,64]{2,1,0:T(8,128)} all-reduce(f32[4,16,64]{2,1,0:T(8,128)S(1)} %fusion.6), channel_id=1, replica_groups=mesh['rows'=8,'ch'=4] {'rows'}, use_global_device_ids=true, to_apply=%region_7.8 | all-reduce | flops 4096 | bytes 32768 | tf_op jit(solution)/shard_map/psum | solution.py:61
  240.8 1.4 convert_element_type.76
  242.1 42.0 %reduce-scatter.11.cloned.1.call-done = f32[16,4,128]{2,0,1:T(8,128)} async-done(((f32[16,32,128]{2,0,1:T(8,128)}), f32[16,4,128]{2,0,1:T(8,128)}) %reduce-scatter.11.cloned.1.call-update) | async-done | bytes 32784 | tf_op jit(solution)/shard_map/reduce_scatter | solution.py:29
  284.2 1.4 fusion.10
  (60 shorter events, 9.7 us)
Async XLA Ops:
  7.2 11.9 %copy-start = (bf16[4,20,128,128]{3,2,1,0:T(8,128)(2,1)S(1)}, bf16[4,20,128,128]{3,2,1,0:T(8,128)(2,1)}, u32[]{:S(2)}) copy-start(bf16[4,20,128,128]{3,2,1,0:T(8,128)(2,1)} %param.7) | copy-start | bytes 7864324
  7.2 123.2 %reduce-scatter.7.cloned.1.call-start = ((), (), s32[]{:S(2)}) async-start(), calls=%async_computation.5 | async-start | bytes 294912 | tf_op jit(solution)/shard_map/reduce_scatter | solution.py:29
  16.9 0.6 copy-start.5
  18.4 0.6 copy-start.4
  19.1 12.7 %copy-start.7 = (bf16[16,512]{1,0:T(8,128)(2,1)S(1)}, bf16[16,512]{1,0:T(8,128)(2,1)}, u32[]{:S(2)}) copy-start(bf16[16,512]{1,0:T(8,128)(2,1)} %param.6) | copy-start | bytes 49156
  28.9 0.7 copy-start.2
  29.7 168.6 %reduce-scatter.9.cloned.1.call-start = ((), (), s32[]{:S(2)}) async-start(), calls=%async_computation.6 | async-start | bytes 294912 | tf_op jit(solution)/shard_map/reduce_scatter | solution.py:29
  135.3 0.7 copy-start.3
  135.3 2.6 copy-start.8
  135.3 2.6 copy-start.10
  135.3 2.6 copy-start.12
  135.3 3.6 %copy-start.6 = (f32[1,16,512]{2,1,0:T(8,128)S(1)}, f32[1,16,512]{2,1,0:T(8,128)}, u32[]{:S(2)}) copy-start(f32[1,16,512]{2,1,0:T(8,128)} %get-tuple-element.3) | copy-start | bytes 98308
  136.0 104.8 %reduce-scatter.5.cloned.1.call-start = ((), (), s32[]{:S(2)}) async-start(), calls=%async_computation.4 | async-start | bytes 163840 | tf_op jit(solution)/shard_map/reduce_scatter | solution.py:53
  137.9 61.6 %copy-start.9 = (bf16[1,16,512]{2,1,0:T(8,128)(2,1)}, bf16[1,16,512]{2,1,0:T(8,128)(2,1)S(1)}, u32[]{:S(2)}) copy-start(bf16[1,16,512]{2,1,0:T(8,128)(2,1)S(1)} %convert_element_type.71) | copy-start | bytes 49156
  137.9 1.0 copy-start.11
  138.8 145.3 %reduce-scatter.11.cloned.1.call-start = ((), (), s32[]{:S(2)}) async-start(), calls=%async_computation.7 | async-start | bytes 294912 | tf_op jit(solution)/shard_map/reduce_scatter | solution.py:29
  203.2 0.7 copy-start.1
Sparse Core Ops, SparseCore 0:
  29.8 62.9 reduce-scatter.6
  136.1 62.0 reduce-scatter.8
  200.7 18.6 reduce-scatter.4
  222.9 61.2 reduce-scatter.10
where the time goes:
time: 293 us; the launch traced here: 292 us
  blocking collectives  135 us (46%)
  waiting for transfers between devices  101 us (34%)
  other arithmetic  23.6 us (8%)
  between operations  14 us (5%)
  local copies, waits for them, and re-layouts  9.28 us (3%)
  matrix products  8.92 us (3%)
    reduce_scatter x3, waiting for transfers between devices, return_partials(): return lax.psum_scatter(partials, 'rows', scatter_dimension=1, tiled=True)  101 us
    all_gather x3, blocking collectives, gather_source(): return lax.all_gather(values, 'rows', axis=1, tiled=True)  92.4 us
    psum x1, blocking collectives, body(): weight_grad = lax.psum(local_wgrad, 'rows')  35.8 us
    scatter-add x3, other arithmetic, transposed_apply(): partials = jnp.zeros((channels, extent, block_width), jnp.float32).at[:,...  11.1 us
    all_gather x1, blocking collectives, body(): grad_out = lax.all_gather(cotangent, 'ch', axis=0, tiled=True)  6.45 us
  transfers between devices with their start and end apart: 4, of which 2 were waited for; matrix products, arithmetic and copies ran while one was open for 6% of the time, Pallas kernels for 0%

commit v1 on v0

--- a/solution.py
+++ b/solution.py
@@ -58,7 +58,11 @@
     ).astype(jnp.bfloat16)
     grad_out = lax.all_gather(cotangent, "ch", axis=0, tiled=True)
     local_wgrad = jnp.einsum("kin,on->kio", stacked, grad_out, preferred_element_type=jnp.float32)
-    weight_grad = lax.psum(local_wgrad, "rows")
+    weight_grad = local_wgrad
+    for hop in (1, 2, 4):
+        weight_grad = weight_grad + lax.ppermute(
+            weight_grad, "rows", [(dev, dev ^ hop) for dev in range(8)]
+        )
     term_grads = jnp.einsum("kio,on->kin", weights, grad_out, preferred_element_type=jnp.float32)
     adjoints = [term_grads[degree] for degree in range(K)]
     for degree in range(K - 1, 1, -1):

time: 293 us -> 292 us (level)
  blocking collectives: 135 us -> 99.1 us
  waiting for transfers between devices: 101 us -> 132 us
  starting transfers between devices: 0.16 us -> 4.47 us
    psum x1 -> x0, blocking collectives: 35.8 us -> none  [body(): weight_grad = lax.psum(local_wgrad, 'rows')]
    reduce_scatter x3, waiting for transfers between devices: 101 us -> 123 us  [return_partials(): return lax.psum_scatter(partials, 'rows', scatter_dimension=1, tiled=True)]
    ppermute x0 -> x3, waiting for transfers between devices: none -> 8.54 us  [body(): lax.ppermute(weight_grad, 'rows', [(dev, dev ^ hop) for dev in range(8)])]
    ppermute x0 -> x3, starting transfers between devices: none -> 4.3 us  [body(): lax.ppermute(weight_grad, 'rows', [(dev, dev ^ hop) for dev in range(8)])]
  transfers between devices with their start and end apart: 4 -> 7, of which waited for: 2 -> 6; matrix products, arithmetic and copies ran while one was open for 6% -> 6% of each run, Pallas kernels for 0% -> 0%
where the time goes in v1:
time: 292 us; the launch traced here: 291 us
  waiting for transfers between devices  132 us (45%)
  blocking collectives  99.1 us (34%)
  other arithmetic  23.4 us (8%)
  between operations  14 us (5%)
  matrix products  8.92 us (3%)
  local copies, waits for them, and re-layouts  8.71 us (3%)
  starting transfers between devices  4.47 us (2%)
    reduce_scatter x3, waiting for transfers between devices, return_partials(): return lax.psum_scatter(partials, 'rows', scatter_dimension=1, tiled=True)  123 us
    all_gather x3, blocking collectives, gather_source(): return lax.all_gather(values, 'rows', axis=1, tiled=True)  92.6 us
    scatter-add x3, other arithmetic, transposed_apply(): partials = jnp.zeros((channels, extent, block_width), jnp.float32).at[:,...  11.1 us
    ppermute x3, waiting for transfers between devices, body(): lax.ppermute(weight_grad, 'rows', [(dev, dev ^ hop) for dev in range(8)])  8.54 us
    all_gather x1, blocking collectives, body(): grad_out = lax.all_gather(cotangent, 'ch', axis=0, tiled=True)  6.45 us
  transfers between devices with their start and end apart: 7, of which 6 were waited for; matrix products, arithmetic and copies ran while one was open for 6% of the time, Pallas kernels for 0%

profile of v1, /device:TPU:0, one launch (start us, length us, event | category | flops | bytes accessed | tf_op | source)
XLA Modules:
  0.0 290.9 jit_solution(10207715777495857900)
XLA Ops:
  7.2 1.6 fusion.37
  10.5 6.4 %all_gather.15 = bf16[64,512]{1,0:T(8,128)(2,1)S(1)} all-gather(bf16[16,512]{1,0:T(8,128)(2,1)} %param.11), channel_id=1, replica_groups=mesh['rows'=8,'ch'=4] {'ch'}, dimensions={0}, use_global_device_ids=true | all-gather | bytes 81920 | tf_op jit(solution)/shard_map/all_gather | solution.py:59
  19.6 5.7 %fusion.30 = s32[80]{0:T(128)} fusion(pred[80,1]{0,1:T(4,128)(4,1)S(1)} %lt.31, s32[80,1]{0,1:T(1,128)S(1)} %add.107, s32[80,1]{0,1:T(1,128)S(1)} %min.12, s32[]{:T(128)} %bitcast.3, s32[]{:T(128)} %bitcast.4, s32[]{:T(128)} %bitcast.5, s32[]{:T(128)} %bitcast.6, s32[]{:T(128)} %bitcast.7, s32[]{:T(128)} %bitcast.9, s32[]{:T(128)} %bitcast.8, s32[]{:T(128)} %bitcast.2), kind=kLoop, calls=%fused_computation.64 | loop fusion | flops 1920 | bytes 1072 | tf_op jit(solution)/shard_map/select_n | solution.py:33
  25.3 3.7 %scatter_fusion = f32[16,32,128]{2,0,1:T(8,128)S(1)} fusion(f32[16,32,128]{2,0,1:T(8,128)S(1)} %broadcast.155.clone, s32[80]{0:T(128)} %fusion.30, f32[80,16,128]{2,1,0:T(8,128)S(1)} %bitcast.172), kind=kCustom, calls=%fused_computation.3 | custom fusion | flops 163840 | bytes 1966400 | tf_op jit(solution)/shard_map/scatter-add | solution.py:44
  30.4 31.4 %all_gather.12 = bf16[16,32,128]{2,0,1:T(8,128)(2,1)S(1)} all-gather(bf16[16,4,128]{2,0,1:T(8,128)(2,1)S(1)} %copy_bitcast_fusion.1), channel_id=1, replica_groups=mesh['rows'=8,'ch'=4] {'rows'}, dimensions={1}, use_global_device_ids=true | all-gather | bytes 147456 | tf_op jit(solution)/shard_map/all_gather | solution.py:26
  63.2 30.7 %all_gather.13 = bf16[16,32,128]{2,0,1:T(8,128)(2,1)S(1)} all-gather(bf16[16,4,128]{2,0,1:T(8,128)(2,1)S(1)} %fusion.5), channel_id=1, replica_groups=mesh['rows'=8,'ch'=4] {'rows'}, dimensions={1}, use_global_device_ids=true | all-gather | bytes 147456 | tf_op jit(solution)/shard_map/all_gather | solution.py:26
  96.6 30.5 %all_gather.14 = bf16[16,32,128]{2,0,1:T(8,128)(2,1)S(1)} all-gather(bf16[16,4,128]{2,0,1:T(8,128)(2,1)S(1)} %bitcast.179), channel_id=1, replica_groups=mesh['rows'=8,'ch'=4] {'rows'}, dimensions={1}, use_global_device_ids=true | all-gather | bytes 147456 | tf_op jit(solution)/shard_map/all_gather | solution.py:26
  127.1 1.4 gather_fusion.2
  129.1 1.2 fusion.16
  130.4 3.7 %scatter_fusion.1 = f32[16,32,128]{2,0,1:T(8,128)S(1)} fusion(f32[16,32,128]{2,0,1:T(8,128)S(1)} %broadcast.155.clone.1, s32[80]{0:T(128)} %fusion.30, f32[80,16,128]{2,1,0:T(8,128)S(1)} %bitcast.171), kind=kCustom, calls=%fused_computation.4 | custom fusion | flops 163840 | bytes 1966400 | tf_op jit(solution)/shard_map/scatter-add | solution.py:44
  134.8 1.7 fusion.1
  137.7 59.3 %reduce-scatter.9.cloned.1.call-done = f32[16,4,128]{2,0,1:T(8,128)} async-done(((f32[16,32,128]{2,0,1:T(8,128)}), f32[16,4,128]{2,0,1:T(8,128)}) %reduce-scatter.9.cloned.1.call-update) | async-done | bytes 32784 | tf_op jit(solution)/shard_map/reduce_scatter | solution.py:29
  197.0 1.2 fusion.19
  198.3 3.7 %scatter_fusion.2 = f32[16,32,128]{2,0,1:T(8,128)S(1)} fusion(f32[16,32,128]{2,0,1:T(8,128)S(1)} %broadcast.155, s32[80]{0:T(128)} %fusion.30, f32[80,16,128]{2,1,0:T(8,128)S(1)} %bitcast.170), kind=kCustom, calls=%fused_computation.5 | custom fusion | flops 163840 | bytes 1966400 | tf_op jit(solution)/shard_map/scatter-add | solution.py:44
  202.7 1.0 fusion.6
  203.7 1.5 collective-permute-start
  205.2 2.5 collective-permute-done
  207.7 1.4 collective-permute-start.1
  209.2 2.6 collective-permute-done.1
  211.8 1.4 collective-permute-start.2
  213.2 3.4 %collective-permute-done.2 = f32[4,16,64]{2,1,0:T(8,128)S(1)} collective-permute-done((f32[4,16,64]{2,1,0:T(8,128)S(1)}, f32[4,16,64]{2,1,0:T(8,128)S(1)}, u32[]{:S(2)}, u32[]{:S(2)}) %collective-permute-start.2) | collective-permute-done | bytes 16416 | tf_op jit(solution)/shard_map/ppermute | solution.py:63
  218.1 1.4 convert_element_type.76
  219.5 63.4 %reduce-scatter.11.cloned.1.call-done = f32[16,4,128]{2,0,1:T(8,128)} async-done(((f32[16,32,128]{2,0,1:T(8,128)}), f32[16,4,128]{2,0,1:T(8,128)}) %reduce-scatter.11.cloned.1.call-update) | async-done | bytes 32784 | tf_op jit(solution)/shard_map/reduce_scatter | solution.py:29
  282.9 1.4 fusion.10
  (70 shorter events, 14.5 us)
Async XLA Ops:
  7.2 11.9 %copy-start = (bf16[4,20,128,128]{3,2,1,0:T(8,128)(2,1)S(1)}, bf16[4,20,128,128]{3,2,1,0:T(8,128)(2,1)}, u32[]{:S(2)}) copy-start(bf16[4,20,128,128]{3,2,1,0:T(8,128)(2,1)} %param.7) | copy-start | bytes 7864324
  7.2 121.9 %reduce-scatter.7.cloned.1.call-start = ((), (), s32[]{:S(2)}) async-start(), calls=%async_computation.5 | async-start | bytes 294912 | tf_op jit(solution)/shard_map/reduce_scatter | solution.py:29
  16.9 0.6 copy-start.6
  18.4 0.7 copy-start.4
  19.1 11.3 %copy-start.8 = (bf16[16,512]{1,0:T(8,128)(2,1)S(1)}, bf16[16,512]{1,0:T(8,128)(2,1)}, u32[]{:S(2)}) copy-start(bf16[16,512]{1,0:T(8,128)(2,1)} %param.6) | copy-start | bytes 49156
  29.0 0.7 copy-start.2
  29.7 167.4 %reduce-scatter.9.cloned.1.call-start = ((), (), s32[]{:S(2)}) async-start(), calls=%async_computation.6 | async-start | bytes 294912 | tf_op jit(solution)/shard_map/reduce_scatter | solution.py:29
  63.2 65.3 %copy-start.5 = (f32[4,16,512]{2,1,0:T(8,128)S(1)}, f32[4,16,512]{2,1,0:T(8,128)}, u32[]{:S(2)}) copy-start(f32[4,16,512]{2,1,0:T(8,128)} %copy-done.4) | copy-start | bytes 393220
  134.1 0.7 copy-start.3
  134.1 2.6 copy-start.9
  134.1 2.6 copy-start.11
  134.1 2.6 copy-start.13
  134.1 3.6 %copy-start.7 = (f32[1,16,512]{2,1,0:T(8,128)S(1)}, f32[1,16,512]{2,1,0:T(8,128)}, u32[]{:S(2)}) copy-start(f32[1,16,512]{2,1,0:T(8,128)} %get-tuple-element.3) | copy-start | bytes 98308
  134.8 83.3 %reduce-scatter.5.cloned.1.call-start = ((), (), s32[]{:S(2)}) async-start(), calls=%async_computation.4 | async-start | bytes 163840 | tf_op jit(solution)/shard_map/reduce_scatter | solution.py:53
  136.7 61.6 %copy-start.10 = (bf16[1,16,512]{2,1,0:T(8,128)(2,1)}, bf16[1,16,512]{2,1,0:T(8,128)(2,1)S(1)}, u32[]{:S(2)}) copy-start(bf16[1,16,512]{2,1,0:T(8,128)(2,1)S(1)} %convert_element_type.71) | copy-start | bytes 49156
  136.7 1.0 copy-start.12
  137.6 145.3 %reduce-scatter.11.cloned.1.call-start = ((), (), s32[]{:S(2)}) async-start(), calls=%async_computation.7 | async-start | bytes 294912 | tf_op jit(solution)/shard_map/reduce_scatter | solution.py:29
  202.0 0.7 copy-start.1
  203.7 4.0 %collective-permute-start = (f32[4,16,64]{2,1,0:T(8,128)S(1)}, f32[4,16,64]{2,1,0:T(8,128)S(1)}, u32[]{:S(2)}, u32[]{:S(2)}) collective-permute-start(f32[4,16,64]{2,1,0:T(8,128)S(1)} %fusion.6), channel_id=1, source_target_pairs={{0,4},{4,0},{8,12},{12,8},{16,20},{20,16},{24,28},{28,24},{1,5},{5... | collective-permute-start | bytes 49160 | tf_op jit(solution)/shard_map/ppermute | solution.py:63
  207.7 4.0 %collective-permute-start.1 = (f32[4,16,64]{2,1,0:T(8,128)S(1)}, f32[4,16,64]{2,1,0:T(8,128)S(1)}, u32[]{:S(2)}, u32[]{:S(2)}) collective-permute-start(f32[4,16,64]{2,1,0:T(8,128)S(1)} %add.116), channel_id=1, source_target_pairs={{0,8},{4,12},{8,0},{12,4},{16,24},{20,28},{24,16},{28,20},{1,9},{5... | collective-permute-start | bytes 49160 | tf_op jit(solution)/shard_map/ppermute | solution.py:63
  211.8 4.8 %collective-permute-start.2 = (f32[4,16,64]{2,1,0:T(8,128)S(1)}, f32[4,16,64]{2,1,0:T(8,128)S(1)}, u32[]{:S(2)}, u32[]{:S(2)}) collective-permute-start(f32[4,16,64]{2,1,0:T(8,128)S(1)} %add.117), channel_id=1, source_target_pairs={{0,16},{4,20},{8,24},{12,28},{16,0},{20,4},{24,8},{28,12},{1,17},{... | collective-permute-start | bytes 49160 | tf_op jit(solution)/shard_map/ppermute | solution.py:63
Sparse Core Ops, SparseCore 0:
  29.8 63.0 reduce-scatter.6
  134.9 62.0 reduce-scatter.8
  199.5 18.6 reduce-scatter.4
  221.7 61.1 reduce-scatter.10
